TPU v7x, 256 devices: a whole 4x4x8 slice. The times are simulated.
256 devices in a mesh: dp: 16 (over y_hi, x, core), seq: 16 (over z, y_lo).
Axes of the slice: x: 4, y: 4 (y_hi: 2, y_lo: 2; y = y_hi * 2 + y_lo), z: 8, core: 2. Of those that a mesh axis runs over, the one named last changes fastest.
Arguments:
- query_rows: bfloat16 [32768, 4096], P(('dp', 'seq')), parts along dimension 0, may hold values from -32 to 32
- key_rows: bfloat16 [32768, 4096], P(('dp', 'seq')), parts along dimension 0, may hold values from -32 to 32
- value_rows: bfloat16 [32768, 4096], P(('dp', 'seq')), parts along dimension 0, may hold values from -6 to 6
- query_tangent: bfloat16 [32768, 4096], P(('dp', 'seq')), parts along dimension 0, may hold values from -6 to 6
- key_tangent: bfloat16 [32768, 4096], P(('dp', 'seq')), parts along dimension 0, may hold values from -6 to 6
- value_tangent: bfloat16 [32768, 4096], P(('dp', 'seq')), parts along dimension 0, may hold values from -6 to 6
Outputs:
- attended: bfloat16 [32768, 4096], P(('dp', 'seq')), parts along dimension 0
- attended_tangent: bfloat16 [32768, 4096], P(('dp', 'seq')), parts along dimension 0
There are 16 independent parts, one for each index of `dp`. A program takes and returns all parts, laid end to end along the dimension named above; each array names one. Nothing has to cross between parts.
All inputs are finite; a program needn't handle non-finite values.
Results may differ from a plain program's by a relative error of at most 0.0049.
Values may be sent and summed in bfloat16 or wider, within the bound.
A program may use at most 64 MiB of HBM per device.

v0:
```python
import math

import jax
import jax.numpy as jnp
from jax import lax
from jax.sharding import PartitionSpec as P

HEADS = 32
HEAD = 128


def sent_together(arrays, axis, split_dim, concat_dim, along):
    widths = [a.shape[along] for a in arrays]
    both = jnp.concatenate(arrays, axis=along)
    result = lax.all_to_all(both, axis, split_axis=split_dim, concat_axis=concat_dim, tiled=True)
    return tuple(jnp.split(result, [sum(widths[:k]) for k in range(1, len(widths))], axis=along))


def attend(head_queries, head_keys, head_values, query_tangent, key_tangent, value_tangent):
    length, head_count, head_width = head_queries.shape
    block_rows = math.gcd(length, 512)
    block_count = length // block_rows
    score_scale = head_width ** (-0.5)
    query_blocks = head_queries.reshape(block_count, block_rows, head_count, head_width)
    tangent_blocks = query_tangent.reshape(block_count, block_rows, head_count, head_width)

    def one_block(pieces):
        query_block, tangent_block = pieces
        scores = (
            jnp.einsum("qhd,khd->hqk", query_block, head_keys, preferred_element_type=jnp.float32)
            * score_scale
        )
        score_tangent = (
            jnp.einsum("qhd,khd->hqk", tangent_block, head_keys, preferred_element_type=jnp.float32)
            + jnp.einsum(
                "qhd,khd->hqk", query_block, key_tangent, preferred_element_type=jnp.float32
            )
        ) * score_scale
        row_max = jnp.max(scores, axis=2, keepdims=True)
        raised = jnp.exp(scores - row_max)
        exact_weights = raised / jnp.sum(raised, axis=2, keepdims=True)
        weights = exact_weights.astype(jnp.bfloat16)
        output = jnp.einsum(
            "hqk,khd->qhd", weights, head_values, preferred_element_type=jnp.float32
        ).astype(jnp.bfloat16)
        mean_tangent = jnp.sum(exact_weights * score_tangent, axis=2, keepdims=True)
        weight_tangent = (exact_weights * (score_tangent - mean_tangent)).astype(jnp.bfloat16)
        tangent = jnp.einsum(
            "hqk,khd->qhd", weight_tangent, head_values, preferred_element_type=jnp.float32
        ) + jnp.einsum("hqk,khd->qhd", weights, value_tangent, preferred_element_type=jnp.float32)
        return (output, tangent.astype(jnp.bfloat16))

    outputs, tangents = lax.map(one_block, (query_blocks, tangent_blocks))
    return (
        outputs.reshape(length, head_count, head_width),
        tangents.reshape(length, head_count, head_width),
    )


def attend_items(pieces):
    flat = tuple((piece[:, 0] for piece in pieces))
    head_output, head_tangent = attend(*flat)
    return (head_output[:, None], head_tangent[:, None])


def on_device(query_rows, key_rows, value_rows, query_tangent, key_tangent, value_tangent):
    local_rows = query_rows.shape[0]
    groups = lax.axis_size("seq")
    per_group = HEADS // groups
    split_queries = query_rows.reshape(local_rows, groups, per_group, HEAD)
    split_keys = key_rows.reshape(local_rows, groups, per_group, HEAD)
    split_values = value_rows.reshape(local_rows, groups, per_group, HEAD)
    split_dquery = query_tangent.reshape(local_rows, groups, per_group, HEAD)
    split_dkey = key_tangent.reshape(local_rows, groups, per_group, HEAD)
    split_dvalue = value_tangent.reshape(local_rows, groups, per_group, HEAD)
    head_queries, head_keys, head_values = (
        lax.all_to_all(split_queries, "seq", split_axis=1, concat_axis=0, tiled=True),
        lax.all_to_all(split_keys, "seq", split_axis=1, concat_axis=0, tiled=True),
        lax.all_to_all(split_values, "seq", split_axis=1, concat_axis=0, tiled=True),
    )
    head_dquery, head_dkey, head_dvalue = sent_together(
        (split_dquery, split_dkey, split_dvalue), "seq", 1, 0, 2
    )
    head_output, head_tangent = attend_items(
        (head_queries, head_keys, head_values, head_dquery, head_dkey, head_dvalue)
    )
    token_output, token_tangent = (
        lax.all_to_all(head_output, "seq", split_axis=0, concat_axis=1, tiled=True),
        lax.all_to_all(head_tangent, "seq", split_axis=0, concat_axis=1, tiled=True),
    )
    attended = token_output.reshape(local_rows, HEADS * HEAD)
    attended_tangent = token_tangent.reshape(local_rows, HEADS * HEAD)
    return (attended, attended_tangent)


def solution(mesh):
    return jax.shard_map(
        on_device,
        mesh=mesh,
        in_specs=(
            P(("dp", "seq"), None),
            P(("dp", "seq"), None),
            P(("dp", "seq"), None),
            P(("dp", "seq"), None),
            P(("dp", "seq"), None),
            P(("dp", "seq"), None),
        ),
        out_specs=(P(("dp", "seq"), None), P(("dp", "seq"), None)),
        check_vma=False,
    )
```

profile of v0, /device:TPU:2, one launch (start us, length us, event | category | flops | bytes accessed | tf_op | source)
XLA Modules:
  0.0 342.6 jit_solution(9685383802823660633)
XLA Ops:
  0.6 1.7 copy.54
  3.7 9.6 %all-to-all-start.1 = ((bf16[128,16,2,128]{3,0,2,1:T(8,128)(2,1)}), bf16[128,16,2,128]{3,0,2,1:T(8,128)(2,1)S(1)}, u32[]{:S(2)}, u32[]{:S(2)}) async-start(bf16[128,16,2,128]{3,0,2,1:T(8,128)(2,1)} %copy.55), calls=%async_computation.1 | async-start | bytes 2097152 | tf_op jit(solution)/shard_map/all_to_all | solution.py:78
  13.3 1.6 copy.57
  16.2 25.8 %all-to-all-done.1 = bf16[128,16,2,128]{3,0,2,1:T(8,128)(2,1)S(1)} async-done(((bf16[128,16,2,128]{3,0,2,1:T(8,128)(2,1)}), bf16[128,16,2,128]{3,0,2,1:T(8,128)(2,1)S(1)}, u32[]{:S(2)}, u32[]{:S(2)}) %all-to-all-start.1) | async-done | bytes 1048608 | tf_op jit(solution)/shard_map/all_to_all | solution.py:78
  42.0 3.7 %all-to-all-start.2 = ((bf16[128,16,2,128]{3,0,2,1:T(8,128)(2,1)}), bf16[128,16,2,128]{3,0,2,1:T(8,128)(2,1)S(1)}, u32[]{:S(2)}, u32[]{:S(2)}) async-start(bf16[128,16,2,128]{3,0,2,1:T(8,128)(2,1)} %copy.58), calls=%async_computation.2 | async-start | bytes 2097152 | tf_op jit(solution)/shard_map/all_to_all | solution.py:79
  47.0 26.5 %all-to-all-done.2 = bf16[128,16,2,128]{3,0,2,1:T(8,128)(2,1)S(1)} async-done(((bf16[128,16,2,128]{3,0,2,1:T(8,128)(2,1)}), bf16[128,16,2,128]{3,0,2,1:T(8,128)(2,1)S(1)}, u32[]{:S(2)}, u32[]{:S(2)}) %all-to-all-start.2) | async-done | bytes 1048608 | tf_op jit(solution)/shard_map/all_to_all | solution.py:79
  73.5 4.3 %all-to-all-start = ((bf16[128,16,2,128]{0,3,2,1:T(8,128)(2,1)}), bf16[128,16,2,128]{0,3,2,1:T(8,128)(2,1)}, u32[]{:S(2)}, u32[]{:S(2)}) async-start(bf16[128,16,2,128]{0,3,2,1:T(8,128)(2,1)} %bitcast.6), calls=%async_computation | async-start | bytes 2097152 | tf_op jit(solution)/shard_map/all_to_all | solution.py:77
  77.8 2.3 copy.60
  80.1 2.3 copy.61
  82.3 2.3 copy.62
  84.6 2.0 pad_maximum_fusion
  86.7 2.8 copy.63
  89.5 15.3 %all-to-all-done = bf16[128,16,2,128]{0,3,2,1:T(8,128)(2,1)} async-done(((bf16[128,16,2,128]{0,3,2,1:T(8,128)(2,1)}), bf16[128,16,2,128]{0,3,2,1:T(8,128)(2,1)}, u32[]{:S(2)}, u32[]{:S(2)}) %all-to-all-start) | async-done | bytes 1048608 | tf_op jit(solution)/shard_map/all_to_all | solution.py:77
  104.8 4.7 %all-to-all-start.3 = ((bf16[128,16,6,128]{3,0,2,1:T(8,128)(2,1)}), bf16[128,16,6,128]{3,0,2,1:T(8,128)(2,1)}, u32[]{:S(2)}, u32[]{:S(2)}) async-start(bf16[128,16,6,128]{3,0,2,1:T(8,128)(2,1)} %copy.63), calls=%async_computation.3 | async-start | bytes 6291456 | tf_op jit(solution)/shard_map/all_to_all | solution.py:15
  109.5 2.3 copy.53
  113.0 68.5 %all-to-all-done.3 = bf16[128,16,6,128]{3,0,2,1:T(8,128)(2,1)} async-done(((bf16[128,16,6,128]{3,0,2,1:T(8,128)(2,1)}), bf16[128,16,6,128]{3,0,2,1:T(8,128)(2,1)}, u32[]{:S(2)}, u32[]{:S(2)}) %all-to-all-start.3) | async-done | bytes 3145760 | tf_op jit(solution)/shard_map/all_to_all | solution.py:15
  181.5 2.3 copy.64
  185.3 87.6 %while.12 = (s32[]{:T(128)}, bf16[4,512,2,128]{3,1,0,2:T(8,128)(2,1)}, bf16[4,512,2,128]{3,1,0,2:T(8,128)(2,1)}, bf16[4,512,2,128]{3,1,0,2:T(8,128)(2,1)S(1)}, b...) while((s32[]{:T(128)}, ...), condition=%wide.region_4.5_spmd, body=%wide.region_0.4_spmd.sunk | while | flops 3255174144 | bytes 130315488 | solution.py:53
  185.3 5.0 %fusion.94 = (f32[2,512]{1,0:T(2,128)S(1)}, f32[2,512,2048]{2,1,0:T(8,128)}) fusion(bf16[2048,2,128]{2,0,1:T(8,128)(2,1)S(1)} %get-tuple-element.206, bf16[4,512,2,128]{3,1,0,2:T(8,128)(2,1)S(1)} %get-tuple-element.205, s32[]{:T(128)} %get-tuple-element.192), kind=kOutput, calls=%fused_computation.41.clone.1 | convolution fusion | flops 543164416 | bytes 9703428 | tf_op jit(solution)/shard_map/while/body/eval_jaxpr/sub | solution.py:40
  191.6 2.5 copy-done.9
  194.1 4.4 %multiply_reduce_fusion.3 = (f32[2,512]{1,0:T(2,128)S(1)}, f32[2,512,2048]{2,1,0:T(8,128)}) fusion(f32[2,512,2048]{2,1,0:T(8,128)S(1)} %copy-done.9, f32[2,512]{1,0:T(2,128)S(1)} %get-tuple-element.179, f32[2,512,2048]{2,1,0:T(8,128)S(1)} %fusion.96, bf16[2048,2,128]{2,0,1:T(8,128)(2,1)S(1)} %copy-done.8, ...), kind=kOutput, calls=%fused_computation.2.clone.1 | convolution fusion | flops 547355648 | bytes 26484740 | tf_op jit(solution)/shard_map/while/body/eval_jaxpr/qhd,khd->hqk/dot_general | solution.py:35
  198.5 4.5 %fusion.97 = f32[2,512,128]{2,1,0:T(8,128)S(1)} fusion(bf16[2048,2,128]{2,0,1:T(8,128)(2,1)S(1)} %copy-done.6, f32[2,512,2048]{2,1,0:T(8,128)} %get-tuple-element.180, f32[2,512]{1,0:T(2,128)S(1)} %get-tuple-element.181, f32[2,512,2048]{2,1,0:T(8,128)S(1)} %copy-done.9, f32[2,512]{1,0:T(2,128)S(1)} %get-tuple-element.179), kind=kOutput, calls=%fused_computation.7.clone.1 | convolution fusion | flops 545259520 | bytes 18358272 | tf_op jit(solution)/shard_map/while/body/eval_jaxpr/hqk,khd->qhd/dot_general | solution.py:48
  203.1 2.1 fusion.98
  205.1 2.1 fusion.95
  207.2 5.0 %fusion.94 = (f32[2,512]{1,0:T(2,128)S(1)}, f32[2,512,2048]{2,1,0:T(8,128)}) fusion(bf16[2048,2,128]{2,0,1:T(8,128)(2,1)S(1)} %get-tuple-element.206, bf16[4,512,2,128]{3,1,0,2:T(8,128)(2,1)S(1)} %get-tuple-element.205, s32[]{:T(128)} %get-tuple-element.192), kind=kOutput, calls=%fused_computation.41.clone.1 | convolution fusion | flops 543164416 | bytes 9703428 | tf_op jit(solution)/shard_map/while/body/eval_jaxpr/sub | solution.py:40
  213.5 2.5 copy-done.9
  216.0 4.4 %multiply_reduce_fusion.3 = (f32[2,512]{1,0:T(2,128)S(1)}, f32[2,512,2048]{2,1,0:T(8,128)}) fusion(f32[2,512,2048]{2,1,0:T(8,128)S(1)} %copy-done.9, f32[2,512]{1,0:T(2,128)S(1)} %get-tuple-element.179, f32[2,512,2048]{2,1,0:T(8,128)S(1)} %fusion.96, bf16[2048,2,128]{2,0,1:T(8,128)(2,1)S(1)} %copy-done.8, ...), kind=kOutput, calls=%fused_computation.2.clone.1 | convolution fusion | flops 547355648 | bytes 26484740 | tf_op jit(solution)/shard_map/while/body/eval_jaxpr/qhd,khd->hqk/dot_general | solution.py:35
  220.4 4.5 %fusion.97 = f32[2,512,128]{2,1,0:T(8,128)S(1)} fusion(bf16[2048,2,128]{2,0,1:T(8,128)(2,1)S(1)} %copy-done.6, f32[2,512,2048]{2,1,0:T(8,128)} %get-tuple-element.180, f32[2,512]{1,0:T(2,128)S(1)} %get-tuple-element.181, f32[2,512,2048]{2,1,0:T(8,128)S(1)} %copy-done.9, f32[2,512]{1,0:T(2,128)S(1)} %get-tuple-element.179), kind=kOutput, calls=%fused_computation.7.clone.1 | convolution fusion | flops 545259520 | bytes 18358272 | tf_op jit(solution)/shard_map/while/body/eval_jaxpr/hqk,khd->qhd/dot_general | solution.py:48
  225.0 2.1 fusion.98
  227.0 2.1 fusion.95
  229.1 5.0 %fusion.94 = (f32[2,512]{1,0:T(2,128)S(1)}, f32[2,512,2048]{2,1,0:T(8,128)}) fusion(bf16[2048,2,128]{2,0,1:T(8,128)(2,1)S(1)} %get-tuple-element.206, bf16[4,512,2,128]{3,1,0,2:T(8,128)(2,1)S(1)} %get-tuple-element.205, s32[]{:T(128)} %get-tuple-element.192), kind=kOutput, calls=%fused_computation.41.clone.1 | convolution fusion | flops 543164416 | bytes 9703428 | tf_op jit(solution)/shard_map/while/body/eval_jaxpr/sub | solution.py:40
  235.4 2.5 copy-done.9
  237.9 4.4 %multiply_reduce_fusion.3 = (f32[2,512]{1,0:T(2,128)S(1)}, f32[2,512,2048]{2,1,0:T(8,128)}) fusion(f32[2,512,2048]{2,1,0:T(8,128)S(1)} %copy-done.9, f32[2,512]{1,0:T(2,128)S(1)} %get-tuple-element.179, f32[2,512,2048]{2,1,0:T(8,128)S(1)} %fusion.96, bf16[2048,2,128]{2,0,1:T(8,128)(2,1)S(1)} %copy-done.8, ...), kind=kOutput, calls=%fused_computation.2.clone.1 | convolution fusion | flops 547355648 | bytes 26484740 | tf_op jit(solution)/shard_map/while/body/eval_jaxpr/qhd,khd->hqk/dot_general | solution.py:35
  242.3 4.5 %fusion.97 = f32[2,512,128]{2,1,0:T(8,128)S(1)} fusion(bf16[2048,2,128]{2,0,1:T(8,128)(2,1)S(1)} %copy-done.6, f32[2,512,2048]{2,1,0:T(8,128)} %get-tuple-element.180, f32[2,512]{1,0:T(2,128)S(1)} %get-tuple-element.181, f32[2,512,2048]{2,1,0:T(8,128)S(1)} %copy-done.9, f32[2,512]{1,0:T(2,128)S(1)} %get-tuple-element.179), kind=kOutput, calls=%fused_computation.7.clone.1 | convolution fusion | flops 545259520 | bytes 18358272 | tf_op jit(solution)/shard_map/while/body/eval_jaxpr/hqk,khd->qhd/dot_general | solution.py:48
  246.9 2.1 fusion.98
  248.9 2.1 fusion.95
  251.0 5.0 %fusion.94 = (f32[2,512]{1,0:T(2,128)S(1)}, f32[2,512,2048]{2,1,0:T(8,128)}) fusion(bf16[2048,2,128]{2,0,1:T(8,128)(2,1)S(1)} %get-tuple-element.206, bf16[4,512,2,128]{3,1,0,2:T(8,128)(2,1)S(1)} %get-tuple-element.205, s32[]{:T(128)} %get-tuple-element.192), kind=kOutput, calls=%fused_computation.41.clone.1 | convolution fusion | flops 543164416 | bytes 9703428 | tf_op jit(solution)/shard_map/while/body/eval_jaxpr/sub | solution.py:40
  257.3 2.5 copy-done.9
  259.8 4.4 %multiply_reduce_fusion.3 = (f32[2,512]{1,0:T(2,128)S(1)}, f32[2,512,2048]{2,1,0:T(8,128)}) fusion(f32[2,512,2048]{2,1,0:T(8,128)S(1)} %copy-done.9, f32[2,512]{1,0:T(2,128)S(1)} %get-tuple-element.179, f32[2,512,2048]{2,1,0:T(8,128)S(1)} %fusion.96, bf16[2048,2,128]{2,0,1:T(8,128)(2,1)S(1)} %copy-done.8, ...), kind=kOutput, calls=%fused_computation.2.clone.1 | convolution fusion | flops 547355648 | bytes 26484740 | tf_op jit(solution)/shard_map/while/body/eval_jaxpr/qhd,khd->hqk/dot_general | solution.py:35
  264.2 4.5 %fusion.97 = f32[2,512,128]{2,1,0:T(8,128)S(1)} fusion(bf16[2048,2,128]{2,0,1:T(8,128)(2,1)S(1)} %copy-done.6, f32[2,512,2048]{2,1,0:T(8,128)} %get-tuple-element.180, f32[2,512]{1,0:T(2,128)S(1)} %get-tuple-element.181, f32[2,512,2048]{2,1,0:T(8,128)S(1)} %copy-done.9, f32[2,512]{1,0:T(2,128)S(1)} %get-tuple-element.179), kind=kOutput, calls=%fused_computation.7.clone.1 | convolution fusion | flops 545259520 | bytes 18358272 | tf_op jit(solution)/shard_map/while/body/eval_jaxpr/hqk,khd->qhd/dot_general | solution.py:48
  268.7 2.1 fusion.98
  270.8 2.1 fusion.95
  272.9 3.6 %copy.68 = bf16[2048,1,2,128]{3,2,1,0:T(2,128)(2,1)} copy(bf16[2048,1,2,128]{3,0,2,1:T(8,128)(2,1)} %bitcast.27) | data formatting | bytes 2097152 | tf_op jit(solution)/shard_map/broadcast_in_dim;reshape | solution.py:63
  276.5 3.9 %all-to-all-start.4 = ((bf16[2048,1,2,128]{3,2,1,0:T(2,128)(2,1)}), bf16[2048,1,2,128]{3,2,1,0:T(2,128)(2,1)S(1)}, u32[]{:S(2)}, u32[]{:S(2)}) async-start(bf16[2048,1,2,128]{3,2,1,0:T(2,128)(2,1)} %copy.68), calls=%async_computation.4 | async-start | bytes 2097152 | tf_op jit(solution)/shard_map/all_to_all | solution.py:88
  280.4 3.6 %copy.72 = bf16[2048,1,2,128]{3,2,1,0:T(2,128)(2,1)} copy(bf16[2048,1,2,128]{3,0,2,1:T(8,128)(2,1)} %bitcast.31) | data formatting | bytes 2097152 | tf_op jit(solution)/shard_map/broadcast_in_dim;reshape | solution.py:63
  284.0 24.9 %all-to-all-done.4 = bf16[2048,1,2,128]{3,2,1,0:T(2,128)(2,1)S(1)} async-done(((bf16[2048,1,2,128]{3,2,1,0:T(2,128)(2,1)}), bf16[2048,1,2,128]{3,2,1,0:T(2,128)(2,1)S(1)}, u32[]{:S(2)}, u32[]{:S(2)}) %all-to-all-start.4) | async-done | bytes 1048608 | tf_op jit(solution)/shard_map/all_to_all | solution.py:88
  308.9 3.7 %all-to-all-start.5 = ((bf16[2048,1,2,128]{3,2,1,0:T(2,128)(2,1)}), bf16[2048,1,2,128]{3,2,1,0:T(2,128)(2,1)S(1)}, u32[]{:S(2)}, u32[]{:S(2)}) async-start(bf16[2048,1,2,128]{3,2,1,0:T(2,128)(2,1)} %copy.72), calls=%async_computation.5 | async-start | bytes 2097152 | tf_op jit(solution)/shard_map/all_to_all | solution.py:89
  314.7 25.8 %all-to-all-done.5 = bf16[2048,1,2,128]{3,2,1,0:T(2,128)(2,1)S(1)} async-done(((bf16[2048,1,2,128]{3,2,1,0:T(2,128)(2,1)}), bf16[2048,1,2,128]{3,2,1,0:T(2,128)(2,1)S(1)}, u32[]{:S(2)}, u32[]{:S(2)}) %all-to-all-start.5) | async-done | bytes 1048608 | tf_op jit(solution)/shard_map/all_to_all | solution.py:89
  (58 shorter events, 15.9 us)
Async XLA Ops:
  0.6 45.0 %copy-start.4 = (bf16[128,4096]{1,0:T(8,128)(2,1)S(1)}, bf16[128,4096]{1,0:T(8,128)(2,1)}, u32[]{:S(2)}) copy-start(bf16[128,4096]{1,0:T(8,128)(2,1)} %param.8) | copy-start | bytes 3145732
  3.7 38.3 %all-to-all-start.1 = ((bf16[128,16,2,128]{3,0,2,1:T(8,128)(2,1)}), bf16[128,16,2,128]{3,0,2,1:T(8,128)(2,1)S(1)}, u32[]{:S(2)}, u32[]{:S(2)}) async-start(bf16[128,16,2,128]{3,0,2,1:T(8,128)(2,1)} %copy.55), calls=%async_computation.1 | async-start | bytes 2097152 | tf_op jit(solution)/shard_map/all_to_all | solution.py:78
  42.0 42.6 %copy-start = (bf16[128,16,2,128]{3,0,2,1:T(8,128)(2,1)}, bf16[128,16,2,128]{3,0,2,1:T(8,128)(2,1)S(1)}, u32[]{:S(2)}) copy-start(bf16[128,16,2,128]{3,0,2,1:T(8,128)(2,1)S(1)} %all-to-all-done.1) | copy-start | bytes 3145732
  42.0 31.5 %all-to-all-start.2 = ((bf16[128,16,2,128]{3,0,2,1:T(8,128)(2,1)}), bf16[128,16,2,128]{3,0,2,1:T(8,128)(2,1)S(1)}, u32[]{:S(2)}, u32[]{:S(2)}) async-start(bf16[128,16,2,128]{3,0,2,1:T(8,128)(2,1)} %copy.58), calls=%async_computation.2 | async-start | bytes 2097152 | tf_op jit(solution)/shard_map/all_to_all | solution.py:79
  73.5 11.2 %copy-start.2 = (bf16[128,16,2,128]{3,0,2,1:T(8,128)(2,1)}, bf16[128,16,2,128]{3,0,2,1:T(8,128)(2,1)S(1)}, u32[]{:S(2)}) copy-start(bf16[128,16,2,128]{3,0,2,1:T(8,128)(2,1)S(1)} %all-to-all-done.2) | copy-start | bytes 3145732
  73.5 31.4 %all-to-all-start = ((bf16[128,16,2,128]{0,3,2,1:T(8,128)(2,1)}), bf16[128,16,2,128]{0,3,2,1:T(8,128)(2,1)}, u32[]{:S(2)}, u32[]{:S(2)}) async-start(bf16[128,16,2,128]{0,3,2,1:T(8,128)(2,1)} %bitcast.6), calls=%async_computation | async-start | bytes 2097152 | tf_op jit(solution)/shard_map/all_to_all | solution.py:77
  89.5 22.3 %copy-start.1 = (bf16[128,16,2,128]{3,0,2,1:T(8,128)(2,1)S(1)}, bf16[128,16,2,128]{3,0,2,1:T(8,128)(2,1)}, u32[]{:S(2)}) copy-start(bf16[128,16,2,128]{3,0,2,1:T(8,128)(2,1)} %copy-done) | copy-start | bytes 3145732
  89.5 22.4 %copy-start.3 = (bf16[128,16,2,128]{3,0,2,1:T(8,128)(2,1)S(1)}, bf16[128,16,2,128]{3,0,2,1:T(8,128)(2,1)}, u32[]{:S(2)}) copy-start(bf16[128,16,2,128]{3,0,2,1:T(8,128)(2,1)} %copy-done.2) | copy-start | bytes 3145732
  104.8 76.6 %all-to-all-start.3 = ((bf16[128,16,6,128]{3,0,2,1:T(8,128)(2,1)}), bf16[128,16,6,128]{3,0,2,1:T(8,128)(2,1)}, u32[]{:S(2)}, u32[]{:S(2)}) async-start(bf16[128,16,6,128]{3,0,2,1:T(8,128)(2,1)} %copy.63), calls=%async_computation.3 | async-start | bytes 6291456 | tf_op jit(solution)/shard_map/all_to_all | solution.py:15
  111.9 73.4 %copy-start.5 = (bf16[16,128,1,2,128]{4,1,0,3,2:T(8,128)(2,1)S(1)}, bf16[16,128,1,2,128]{4,1,0,3,2:T(8,128)(2,1)}, u32[]{:S(2)}) copy-start(bf16[16,128,1,2,128]{4,1,0,3,2:T(8,128)(2,1)} %copy.53) | copy-start | bytes 3145732
  190.3 1.3 copy-start.8
  190.3 3.7 %copy-start.9 = (f32[2,512,2048]{2,1,0:T(8,128)S(1)}, f32[2,512,2048]{2,1,0:T(8,128)}, u32[]{:S(2)}) copy-start(f32[2,512,2048]{2,1,0:T(8,128)} %get-tuple-element.178) | copy-start | bytes 25165828 | tf_op jit(solution)/shard_map/while
  194.1 4.4 %copy-start.6 = (bf16[2048,2,128]{2,0,1:T(8,128)(2,1)S(1)}, bf16[2048,2,128]{2,0,1:T(8,128)(2,1)}, u32[]{:S(2)}) copy-start(bf16[2048,2,128]{2,0,1:T(8,128)(2,1)} %get-tuple-element.207) | copy-start | bytes 3145732 | tf_op jit(solution)/shard_map/while
  198.5 4.5 %copy-start.7 = (bf16[2048,2,128]{2,0,1:T(8,128)(2,1)S(1)}, bf16[2048,2,128]{2,0,1:T(8,128)(2,1)}, u32[]{:S(2)}) copy-start(bf16[2048,2,128]{2,0,1:T(8,128)(2,1)} %get-tuple-element.210) | copy-start | bytes 3145732 | tf_op jit(solution)/shard_map/while
  212.2 1.3 copy-start.8
  212.2 3.7 %copy-start.9 = (f32[2,512,2048]{2,1,0:T(8,128)S(1)}, f32[2,512,2048]{2,1,0:T(8,128)}, u32[]{:S(2)}) copy-start(f32[2,512,2048]{2,1,0:T(8,128)} %get-tuple-element.178) | copy-start | bytes 25165828 | tf_op jit(solution)/shard_map/while
  216.0 4.4 %copy-start.6 = (bf16[2048,2,128]{2,0,1:T(8,128)(2,1)S(1)}, bf16[2048,2,128]{2,0,1:T(8,128)(2,1)}, u32[]{:S(2)}) copy-start(bf16[2048,2,128]{2,0,1:T(8,128)(2,1)} %get-tuple-element.207) | copy-start | bytes 3145732 | tf_op jit(solution)/shard_map/while
  220.4 4.5 %copy-start.7 = (bf16[2048,2,128]{2,0,1:T(8,128)(2,1)S(1)}, bf16[2048,2,128]{2,0,1:T(8,128)(2,1)}, u32[]{:S(2)}) copy-start(bf16[2048,2,128]{2,0,1:T(8,128)(2,1)} %get-tuple-element.210) | copy-start | bytes 3145732 | tf_op jit(solution)/shard_map/while
  234.1 1.3 copy-start.8
  234.1 3.7 %copy-start.9 = (f32[2,512,2048]{2,1,0:T(8,128)S(1)}, f32[2,512,2048]{2,1,0:T(8,128)}, u32[]{:S(2)}) copy-start(f32[2,512,2048]{2,1,0:T(8,128)} %get-tuple-element.178) | copy-start | bytes 25165828 | tf_op jit(solution)/shard_map/while
  237.9 4.4 %copy-start.6 = (bf16[2048,2,128]{2,0,1:T(8,128)(2,1)S(1)}, bf16[2048,2,128]{2,0,1:T(8,128)(2,1)}, u32[]{:S(2)}) copy-start(bf16[2048,2,128]{2,0,1:T(8,128)(2,1)} %get-tuple-element.207) | copy-start | bytes 3145732 | tf_op jit(solution)/shard_map/while
  242.3 4.5 %copy-start.7 = (bf16[2048,2,128]{2,0,1:T(8,128)(2,1)S(1)}, bf16[2048,2,128]{2,0,1:T(8,128)(2,1)}, u32[]{:S(2)}) copy-start(bf16[2048,2,128]{2,0,1:T(8,128)(2,1)} %get-tuple-element.210) | copy-start | bytes 3145732 | tf_op jit(solution)/shard_map/while
  256.0 1.3 copy-start.8
  256.0 3.7 %copy-start.9 = (f32[2,512,2048]{2,1,0:T(8,128)S(1)}, f32[2,512,2048]{2,1,0:T(8,128)}, u32[]{:S(2)}) copy-start(f32[2,512,2048]{2,1,0:T(8,128)} %get-tuple-element.178) | copy-start | bytes 25165828 | tf_op jit(solution)/shard_map/while
  259.8 4.4 %copy-start.6 = (bf16[2048,2,128]{2,0,1:T(8,128)(2,1)S(1)}, bf16[2048,2,128]{2,0,1:T(8,128)(2,1)}, u32[]{:S(2)}) copy-start(bf16[2048,2,128]{2,0,1:T(8,128)(2,1)} %get-tuple-element.207) | copy-start | bytes 3145732 | tf_op jit(solution)/shard_map/while
  264.2 4.5 %copy-start.7 = (bf16[2048,2,128]{2,0,1:T(8,128)(2,1)S(1)}, bf16[2048,2,128]{2,0,1:T(8,128)(2,1)}, u32[]{:S(2)}) copy-start(bf16[2048,2,128]{2,0,1:T(8,128)(2,1)} %get-tuple-element.210) | copy-start | bytes 3145732 | tf_op jit(solution)/shard_map/while
  276.5 32.4 %all-to-all-start.4 = ((bf16[2048,1,2,128]{3,2,1,0:T(2,128)(2,1)}), bf16[2048,1,2,128]{3,2,1,0:T(2,128)(2,1)S(1)}, u32[]{:S(2)}, u32[]{:S(2)}) async-start(bf16[2048,1,2,128]{3,2,1,0:T(2,128)(2,1)} %copy.68), calls=%async_computation.4 | async-start | bytes 2097152 | tf_op jit(solution)/shard_map/all_to_all | solution.py:88
  308.9 31.6 %all-to-all-start.5 = ((bf16[2048,1,2,128]{3,2,1,0:T(2,128)(2,1)}), bf16[2048,1,2,128]{3,2,1,0:T(2,128)(2,1)S(1)}, u32[]{:S(2)}, u32[]{:S(2)}) async-start(bf16[2048,1,2,128]{3,2,1,0:T(2,128)(2,1)} %copy.72), calls=%async_computation.5 | async-start | bytes 2097152 | tf_op jit(solution)/shard_map/all_to_all | solution.py:89
where the time goes:
time: 343 us
  waiting for transfers between devices  187 us (55%)
  matrix products  77.5 us (23%)
  local copies, waits for them, and re-layouts  45.6 us (13%)
  starting transfers between devices  29.8 us (9%)
    all_to_all x1, waiting for transfers between devices, sent_together(): lax.all_to_all(both, axis, split_axis=split_dim, concat_axis=concat_dim,...  68.5 us
    all_to_all x1, waiting for transfers between devices, on_device(): lax.all_to_all(split_values, 'seq', split_axis=1, concat_axis=0, tiled=True)  26.5 us
    all_to_all x1, waiting for transfers between devices, on_device(): lax.all_to_all(split_keys, 'seq', split_axis=1, concat_axis=0, tiled=True)  25.8 us
    all_to_all x1, waiting for transfers between devices, on_device(): lax.all_to_all(head_tangent, 'seq', split_axis=0, concat_axis=1, tiled=True)  25.8 us
    all_to_all x1, waiting for transfers between devices, on_device(): lax.all_to_all(head_output, 'seq', split_axis=0, concat_axis=1, tiled=True)  24.9 us
    sub x4, matrix products, one_block(): raised = jnp.exp(scores - row_max)  20.1 us
    dot_general x4, matrix products, one_block(): jnp.einsum('hqk,khd->qhd', weight_tangent, head_values, preferred_element...  18.1 us
    dot_general x4, matrix products, one_block(): jnp.einsum('qhd,khd->hqk', query_block, key_tangent, preferred_element_ty...  17.7 us
  transfers between devices with their start and end apart: 6, of which 6 were waited for; matrix products, arithmetic and copies ran while one was open for 7% of the time, Pallas kernels for 0%

commit v1 on v0

v1 whole, which is shorter than its diff:
```python
import functools
import math

import jax
import jax.numpy as jnp
from jax import lax
from jax.experimental import pallas as pl
from jax.experimental.pallas import tpu as pltpu
from jax.sharding import PartitionSpec as P

HEADS = 32
HEAD = 128
MESH_ID = pl.DeviceIdType.MESH
NT = (((1,), (1,)), ((), ()))
NN = (((1,), (0,)), ((), ()))


def kernel(
    groups,
    q_ref,
    k_ref,
    v_ref,
    dq_ref,
    dk_ref,
    dv_ref,
    out_ref,
    dout_ref,
    held,
    result,
    in_send,
    in_recv,
    out_send,
    out_recv,
):
    me = lax.axis_index("seq")
    rows = q_ref.shape[0]
    per_group = HEADS // groups
    steps = groups // 2
    pair = 2 * rows
    scale = HEAD ** (-0.5)
    my_z, my_y = me // 2, me % 2

    def far_first(i):
        distance = (steps - i) // 2
        sign = 2 * (i % 2) - 1
        return lax.rem(my_z + sign * distance + steps, steps)

    barrier = pltpu.get_barrier_semaphore()

    def greet(j, carry):
        pl.semaphore_signal(
            barrier, inc=1, device_id={"seq": lax.rem(me + j, groups)}, device_id_type=MESH_ID
        )
        return carry

    lax.fori_loop(1, groups, greet, 0)

    plan = ((k_ref, 1, 0), (dk_ref, 1, HEAD), (dq_ref, 0, 0), (q_ref, 0, HEAD), (v_ref, 2, 0), (dv_ref, 2, HEAD))

    def piece(source, kind, column, h, peer):
        src = source.at[:, pl.ds(pl.multiple_of((peer * per_group + h) * HEAD, HEAD), HEAD)]
        dst = held.at[h, kind, pl.ds(pl.multiple_of(me * rows, rows), rows), pl.ds(column, HEAD)]
        return src, dst

    for h in range(per_group):
        for source, kind, column in plan:
            src, dst = piece(source, kind, column, h, me)
            pltpu.make_async_copy(src, dst, in_recv.at[h]).start()

    pl.semaphore_wait(barrier, groups - 1)

    for h in range(per_group):

        def send_to(j, carry, h=h):
            peer = far_first(j // 2) * 2 + lax.rem(my_y + j + 1, 2)
            for source, kind, column in plan:
                src, dst = piece(source, kind, column, h, peer)
                pltpu.make_async_remote_copy(
                    src_ref=src,
                    dst_ref=dst,
                    send_sem=in_send,
                    recv_sem=in_recv.at[h],
                    device_id={"seq": peer},
                    device_id_type=MESH_ID,
                ).start()
            return carry

        lax.fori_loop(0, groups - 1, send_to, 0)

    def give(g, target_y, own):
        h, z = g // steps, far_first(g % steps)
        target = z * 2 + target_y
        for part, ref in ((0, out_ref), (1, dout_ref)):
            src = result.at[h, pl.ds(pl.multiple_of(target * rows, rows), rows), pl.ds(part * HEAD, HEAD)]
            dst = ref.at[:, pl.ds(pl.multiple_of((me * per_group + h) * HEAD, HEAD), HEAD)]
            if own:
                pltpu.make_async_copy(src, dst, out_recv.at[part]).start()
            else:
                pltpu.make_async_remote_copy(
                    src_ref=src,
                    dst_ref=dst,
                    send_sem=out_send,
                    recv_sem=out_recv.at[part],
                    device_id={"seq": target},
                    device_id_type=MESH_ID,
                ).start()

    def give_block(g):
        give(g, 1 - my_y, False)

        @pl.when(g % steps == steps - 1)
        def _():
            give(g, my_y, True)

        @pl.when(g % steps != steps - 1)
        def _():
            give(g, my_y, False)

    def block(g, carry):
        h = g // steps

        @pl.when(g % steps == 0)
        def _():
            pltpu.make_async_copy(held.at[h], held.at[h], in_recv.at[h]).wait()

        @pl.when(g > 0)
        def _():
            give_block(g - 1)

        where = pl.ds(pl.multiple_of(far_first(g % steps) * pair, pair), pair)
        both = held[h, 0, where, :]
        keys = held[h, 1]
        values = held[h, 2]
        scores = lax.dot_general(both[:, HEAD:], keys[:, :HEAD], NT, preferred_element_type=jnp.float32)
        tangent = lax.dot_general(both, keys, NT, preferred_element_type=jnp.float32)
        row_max = jnp.max(scores, axis=1, keepdims=True)
        raised = jnp.exp2((scores - row_max) * (scale * math.log2(math.e)))
        inverse = 1.0 / jnp.sum(raised, axis=1, keepdims=True)
        exact = raised * inverse
        mean = jnp.sum(exact * tangent, axis=1, keepdims=True)
        weights = exact.astype(jnp.bfloat16)
        turned = (exact * (tangent - mean)).astype(jnp.bfloat16)
        plain = lax.dot_general(weights, values, NN, preferred_element_type=jnp.float32)
        moved = lax.dot_general(turned, values[:, :HEAD], NN, preferred_element_type=jnp.float32)
        result[h, where, :HEAD] = plain[:, :HEAD].astype(jnp.bfloat16)
        result[h, where, HEAD:] = (moved * scale + plain[:, HEAD:]).astype(jnp.bfloat16)
        return carry

    last = per_group * steps - 1
    lax.fori_loop(0, last + 1, block, 0)
    sent = held.at[:, :, pl.ds(0, (groups - 1) * rows), :]
    pltpu.make_async_copy(sent, sent, in_send).wait()
    give_block(last)
    given = result.at[:, pl.ds(0, (groups - 1) * rows), :]
    pltpu.make_async_copy(given, given, out_send).wait()
    pltpu.make_async_copy(out_ref, out_ref, out_recv.at[0]).wait()
    pltpu.make_async_copy(dout_ref, dout_ref, out_recv.at[1]).wait()


def on_device(*args):
    groups = lax.axis_size("seq")
    per_group = HEADS // groups
    tokens = args[0].shape[0] * groups
    shape = jax.ShapeDtypeStruct(args[0].shape, jnp.bfloat16)
    return pl.pallas_call(
        functools.partial(kernel, groups),
        out_shape=(shape, shape),
        in_specs=[pl.BlockSpec(memory_space=pl.ANY)] * 6,
        out_specs=(pl.BlockSpec(memory_space=pl.ANY),) * 2,
        scratch_shapes=[
            pltpu.VMEM((per_group, 3, tokens, 2 * HEAD), jnp.bfloat16),
            pltpu.VMEM((per_group, tokens, 2 * HEAD), jnp.bfloat16),
            pltpu.SemaphoreType.DMA,
            pltpu.SemaphoreType.DMA((per_group,)),
            pltpu.SemaphoreType.DMA,
            pltpu.SemaphoreType.DMA((2,)),
        ],
        compiler_params=pltpu.CompilerParams(collective_id=0, has_side_effects=True),
        name="attention_tangent",
    )(*args)


def solution(mesh):
    spec = P(("dp", "seq"), None)
    return jax.shard_map(
        on_device, mesh=mesh, in_specs=(spec,) * 6, out_specs=(spec, spec), check_vma=False
    )
```

time: 343 us -> 199 us (0.58)
  Pallas kernels: 0 us -> 195 us
  waiting for transfers between devices: 187 us -> 0 us
  matrix products: 77.5 us -> 0 us
  local copies, waits for them, and re-layouts: 45.6 us -> 3.35 us
  starting transfers between devices: 29.8 us -> 0 us
    pallas_call x0 -> x1, Pallas kernels: none -> 195 us  [on_device(): pl.pallas_call(functools.partial(kernel, groups), out_shape=(shape, shape...]
    all_to_all x6 -> x0, waiting for transfers between devices: 187 us -> none  [the longest x1 68.5 us: sent_together(): lax.all_to_all(both, axis, split_axis=split_dim, concat_axis=concat_dim,...]
    dot_general x20 -> x0, matrix products: 57.3 us -> none  [the longest x4 18.1 us: one_block(): jnp.einsum('hqk,khd->qhd', weight_tangent, head_values, preferred_element...]
    all_to_all x6 -> x0, starting transfers between devices: 29.8 us -> none  [the longest x1 9.58 us: on_device(): lax.all_to_all(split_keys, 'seq', split_axis=1, concat_axis=0, tiled=True)]
    sub x4 -> x0, matrix products: 20.1 us -> none  [one_block(): raised = jnp.exp(scores - row_max)]
    unnamed x20 -> x4, local copies, waits for them, and re-layouts: 14.1 us -> 3.35 us
    while x32 -> x0, local copies, waits for them, and re-layouts: 9.97 us -> none
    all_to_all x8 -> x0, local copies, waits for them, and re-layouts: 7.33 us -> none  [the longest x1 2.29 us: sent_together(): lax.all_to_all(both, axis, split_axis=split_dim, concat_axis=concat_dim,...]
  transfers between devices with their start and end apart: 6 -> 0, of which waited for: 6 -> 0; matrix products, arithmetic and copies ran while one was open for 7% -> 0% of each run, Pallas kernels for 0% -> 0%
where the time goes in v1:
time: 199 us
  Pallas kernels  195 us (98%)
  local copies, waits for them, and re-layouts  3.35 us (2%)
    pallas_call x1, Pallas kernels, on_device(): pl.pallas_call(functools.partial(kernel, groups), out_shape=(shape, shape...  195 us

profile of v1, /device:TPU:2, one launch (start us, length us, event | category | flops | bytes accessed | tf_op | source)
XLA Modules:
  0.0 198.5 jit_solution(3919322475069093423)
XLA Ops:
  0.6 194.5 %attention_tangent.1 = (bf16[128,4096]{1,0:T(8,128)(2,1)}, bf16[128,4096]{1,0:T(8,128)(2,1)}) custom-call(bf16[128,4096]{1,0:T(8,128)(2,1)} %q_ref.1, bf16[128,4096]{1,0:T(8,128)(2,1)} %k_ref.1, bf16[128,4096]{1,0:T(8,128)(2,1)} %v_ref.1, bf16[128,4096]{1,0:T(8,128)(2,1)} %dq_ref.1, bf16[128,4096]{1,0:T(8,128)(2,1)} %dk_ref.1, bf16[128,4096]{1,0:T(8,128)(2,1)} %dv_ref.1), custom_call_target="tpu_custom_call" | custom-call | tf_op jit(solution)/shard_map/attention_tangent/pallas_call | solution.py:165
  195.2 0.0 copy-start
  195.2 2.4 %copy.10 = bf16[128,4096]{1,0:T(8,128)(2,1)} copy(bf16[128,4096]{1,0:T(8,128)(2,1)} %get-tuple-element.4) | data formatting | bytes 2097152
  197.5 0.0 copy-done
  197.5 1.0 copy.11
Async XLA Ops:
  195.2 2.4 %copy-start = (bf16[128,4096]{1,0:T(8,128)(2,1)S(1)}, bf16[128,4096]{1,0:T(8,128)(2,1)}, u32[]{:S(2)}) copy-start(bf16[128,4096]{1,0:T(8,128)(2,1)} %get-tuple-element.5) | copy-start | bytes 3145732

commit v2 on v1

--- a/solution.py
+++ b/solution.py
@@ -31,6 +31,7 @@
     in_recv,
     out_send,
     out_recv,
+    rounds,
 ):
     me = lax.axis_index("seq")
     rows = q_ref.shape[0]
@@ -45,15 +46,13 @@
         sign = 2 * (i % 2) - 1
         return lax.rem(my_z + sign * distance + steps, steps)
 
+    def at(distance, y):
+        return lax.rem(my_z + distance + steps, steps) * 2 + y
+
+    neighbours = (at(1, my_y), at(-1, my_y))
     barrier = pltpu.get_barrier_semaphore()
-
-    def greet(j, carry):
-        pl.semaphore_signal(
-            barrier, inc=1, device_id={"seq": lax.rem(me + j, groups)}, device_id_type=MESH_ID
-        )
-        return carry
-
-    lax.fori_loop(1, groups, greet, 0)
+    for peer in neighbours + (at(0, 1 - my_y),):
+        pl.semaphore_signal(barrier, inc=1, device_id={"seq": peer}, device_id_type=MESH_ID)
 
     plan = ((k_ref, 1, 0), (dk_ref, 1, HEAD), (dq_ref, 0, 0), (q_ref, 0, HEAD), (v_ref, 2, 0), (dv_ref, 2, HEAD))
 
@@ -67,25 +66,41 @@
             src, dst = piece(source, kind, column, h, me)
             pltpu.make_async_copy(src, dst, in_recv.at[h]).start()
 
-    pl.semaphore_wait(barrier, groups - 1)
-
-    for h in range(per_group):
-
-        def send_to(j, carry, h=h):
-            peer = far_first(j // 2) * 2 + lax.rem(my_y + j + 1, 2)
-            for source, kind, column in plan:
-                src, dst = piece(source, kind, column, h, peer)
-                pltpu.make_async_remote_copy(
-                    src_ref=src,
-                    dst_ref=dst,
-                    send_sem=in_send,
-                    recv_sem=in_recv.at[h],
-                    device_id={"seq": peer},
-                    device_id_type=MESH_ID,
-                ).start()
+    def send_to(h, peer):
+        for source, kind, column in plan:
+            src, dst = piece(source, kind, column, h, peer)
+            pltpu.make_async_remote_copy(
+                src_ref=src,
+                dst_ref=dst,
+                send_sem=in_send,
+                recv_sem=in_recv.at[h],
+                device_id={"seq": peer},
+                device_id_type=MESH_ID,
+            ).start()
+
+    pl.semaphore_wait(barrier, 3)
+    half = steps // 2
+    for hops in range(1, half + 2):
+        if hops > 1:
+            for peer in neighbours:
+                pl.semaphore_signal(
+                    rounds.at[hops - 2], inc=1, device_id={"seq": peer}, device_id_type=MESH_ID
+                )
+            pl.semaphore_wait(rounds.at[hops - 2], 2)
+        for distance, y in ((hops - 1, 1 - my_y), (hops, my_y)):
+            if distance <= half:
+                for sign in (1, -1) if 0 < distance < half else (1,):
+                    send_to(0, at(sign * distance, y))
+
+    for h in range(1, per_group):
+
+        def send_rest(j, carry, h=h):
+            i = groups - 2 - j
+            peer = far_first(i // 2) * 2 + lax.rem(my_y + i + 1, 2)
+            send_to(h, peer)
             return carry
 
-        lax.fori_loop(0, groups - 1, send_to, 0)
+        lax.fori_loop(0, groups - 1, send_rest, 0)
 
     def give(g, target_y, own):
         h, z = g // steps, far_first(g % steps)
@@ -157,14 +172,25 @@
     pltpu.make_async_copy(dout_ref, dout_ref, out_recv.at[1]).wait()
 
 
+def put_out(a_ref, b_ref, a_out, b_out, sems):
+    copies = [
+        pltpu.make_async_copy(a_ref, a_out, sems.at[0]),
+        pltpu.make_async_copy(b_ref, b_out, sems.at[1]),
+    ]
+    for copy in copies:
+        copy.start()
+    for copy in copies:
+        copy.wait()
+
+
 def on_device(*args):
     groups = lax.axis_size("seq")
     per_group = HEADS // groups
     tokens = args[0].shape[0] * groups
     shape = jax.ShapeDtypeStruct(args[0].shape, jnp.bfloat16)
-    return pl.pallas_call(
+    landed = pl.pallas_call(
         functools.partial(kernel, groups),
-        out_shape=(shape, shape),
+        out_shape=(pltpu.VMEM(args[0].shape, jnp.bfloat16),) * 2,
         in_specs=[pl.BlockSpec(memory_space=pl.ANY)] * 6,
         out_specs=(pl.BlockSpec(memory_space=pl.ANY),) * 2,
         scratch_shapes=[
@@ -174,10 +200,19 @@
             pltpu.SemaphoreType.DMA((per_group,)),
             pltpu.SemaphoreType.DMA,
             pltpu.SemaphoreType.DMA((2,)),
+            pltpu.SemaphoreType.REGULAR((groups // 4,)),
         ],
         compiler_params=pltpu.CompilerParams(collective_id=0, has_side_effects=True),
         name="attention_tangent",
     )(*args)
+    return pl.pallas_call(
+        put_out,
+        out_shape=(shape, shape),
+        in_specs=[pl.BlockSpec(memory_space=pl.ANY)] * 2,
+        out_specs=(pl.BlockSpec(memory_space=pl.ANY),) * 2,
+        scratch_shapes=[pltpu.SemaphoreType.DMA((2,))],
+        name="put_out",
+    )(*(pltpu.with_memory_space_constraint(x, pltpu.VMEM) for x in landed))
 
 
 def solution(mesh):

time: 199 us -> 191 us (0.960)
  Pallas kernels: 195 us -> 190 us
  local copies, waits for them, and re-layouts: 3.35 us -> 0 us
    pallas_call x1 -> x2, Pallas kernels: 195 us -> 190 us  [the longest x1 189 us: on_device(): pl.pallas_call(functools.partial(kernel, groups), out_shape=(pltpu.VMEM(a...]
    unnamed x4 -> x0, local copies, waits for them, and re-layouts: 3.35 us -> none
where the time goes in v2:
time: 191 us
  Pallas kernels  190 us (99%)
    pallas_call x1, Pallas kernels, on_device(): pl.pallas_call(functools.partial(kernel, groups), out_shape=(pltpu.VMEM(a...  189 us

profile of v2, /device:TPU:2, one launch (start us, length us, event | category | flops | bytes accessed | tf_op | source)
XLA Modules:
  0.0 191.1 jit_solution(5424490510203514607)
XLA Ops:
  0.6 189.1 %attention_tangent.1 = (bf16[128,4096]{1,0:T(8,128)(2,1)S(1)}, bf16[128,4096]{1,0:T(8,128)(2,1)S(1)}) custom-call(bf16[128,4096]{1,0:T(8,128)(2,1)} %q_ref.1, bf16[128,4096]{1,0:T(8,128)(2,1)} %k_ref.1, bf16[128,4096]{1,0:T(8,128)(2,1)} %v_ref.1, bf16[128,4096]{1,0:T(8,128)(2,1)} %dq_ref.1, bf16[128,4096]{1,0:T(8,128)(2,1)} %dk_ref.1, bf16[128,4096]{1,0:T(8,128)(2,1)} %dv_ref.1), custom_call_target="tpu_custom_call" | custom-call | tf_op jit(solution)/shard_map/attention_tangent/pallas_call | solution.py:191
  189.7 1.3 put_out.1

commit v3 on v2

--- a/solution.py
+++ b/solution.py
@@ -1,5 +1,4 @@
 import functools
-import math
 
 import jax
 import jax.numpy as jnp
@@ -66,8 +65,8 @@
             src, dst = piece(source, kind, column, h, me)
             pltpu.make_async_copy(src, dst, in_recv.at[h]).start()
 
-    def send_to(h, peer):
-        for source, kind, column in plan:
+    def send_to(h, peer, part=plan):
+        for source, kind, column in part:
             src, dst = piece(source, kind, column, h, peer)
             pltpu.make_async_remote_copy(
                 src_ref=src,
@@ -93,14 +92,15 @@
                     send_to(0, at(sign * distance, y))
 
     for h in range(1, per_group):
-
-        def send_rest(j, carry, h=h):
-            i = groups - 2 - j
-            peer = far_first(i // 2) * 2 + lax.rem(my_y + i + 1, 2)
-            send_to(h, peer)
-            return carry
-
-        lax.fori_loop(0, groups - 1, send_rest, 0)
+        for entry in plan:
+
+            def send_rest(j, carry, h=h, entry=entry):
+                i = j
+                peer = far_first(i // 2) * 2 + lax.rem(my_y + i + 1, 2)
+                send_to(h, peer, (entry,))
+                return carry
+
+            lax.fori_loop(0, groups - 1, send_rest, 0)
 
     def give(g, target_y, own):
         h, z = g // steps, far_first(g % steps)
@@ -146,10 +146,12 @@
         both = held[h, 0, where, :]
         keys = held[h, 1]
         values = held[h, 2]
-        scores = lax.dot_general(both[:, HEAD:], keys[:, :HEAD], NT, preferred_element_type=jnp.float32)
-        tangent = lax.dot_general(both, keys, NT, preferred_element_type=jnp.float32)
+        scores = scale * lax.dot_general(
+            both[:, HEAD:], keys[:, :HEAD], NT, preferred_element_type=jnp.float32
+        )
+        tangent = scale * lax.dot_general(both, keys, NT, preferred_element_type=jnp.float32)
         row_max = jnp.max(scores, axis=1, keepdims=True)
-        raised = jnp.exp2((scores - row_max) * (scale * math.log2(math.e)))
+        raised = jnp.exp(scores - row_max)
         inverse = 1.0 / jnp.sum(raised, axis=1, keepdims=True)
         exact = raised * inverse
         mean = jnp.sum(exact * tangent, axis=1, keepdims=True)
@@ -158,7 +160,7 @@
         plain = lax.dot_general(weights, values, NN, preferred_element_type=jnp.float32)
         moved = lax.dot_general(turned, values[:, :HEAD], NN, preferred_element_type=jnp.float32)
         result[h, where, :HEAD] = plain[:, :HEAD].astype(jnp.bfloat16)
-        result[h, where, HEAD:] = (moved * scale + plain[:, HEAD:]).astype(jnp.bfloat16)
+        result[h, where, HEAD:] = (moved + plain[:, HEAD:]).astype(jnp.bfloat16)
         return carry
 
     last = per_group * steps - 1

time: 191 us -> 190 us (level)
  no operation moved by 1% of the time
where the time goes in v3:
time: 190 us
  Pallas kernels  190 us (100%)
    pallas_call x1, Pallas kernels, on_device(): pl.pallas_call(functools.partial(kernel, groups), out_shape=(pltpu.VMEM(a...  188 us

profile of v3, /device:TPU:2, one launch (start us, length us, event | category | flops | bytes accessed | tf_op | source)
XLA Modules:
  0.0 190.3 jit_solution(16358033440910505667)
XLA Ops:
  0.6 188.3 %attention_tangent.1 = (bf16[128,4096]{1,0:T(8,128)(2,1)S(1)}, bf16[128,4096]{1,0:T(8,128)(2,1)S(1)}) custom-call(bf16[128,4096]{1,0:T(8,128)(2,1)} %q_ref.1, bf16[128,4096]{1,0:T(8,128)(2,1)} %k_ref.1, bf16[128,4096]{1,0:T(8,128)(2,1)} %v_ref.1, bf16[128,4096]{1,0:T(8,128)(2,1)} %dq_ref.1, bf16[128,4096]{1,0:T(8,128)(2,1)} %dk_ref.1, bf16[128,4096]{1,0:T(8,128)(2,1)} %dv_ref.1), custom_call_target="tpu_custom_call" | custom-call | tf_op jit(solution)/shard_map/attention_tangent/pallas_call | solution.py:193
  188.9 1.3 put_out.1

commit v4 on v3

--- a/solution.py
+++ b/solution.py
@@ -95,8 +95,7 @@
         for entry in plan:
 
             def send_rest(j, carry, h=h, entry=entry):
-                i = j
-                peer = far_first(i // 2) * 2 + lax.rem(my_y + i + 1, 2)
+                peer = far_first(j // 2) * 2 + lax.rem(my_y + j + 1, 2)
                 send_to(h, peer, (entry,))
                 return carry
 
@@ -131,16 +130,14 @@
         def _():
             give(g, my_y, False)
 
+    kept = steps - 3
+
     def block(g, carry):
         h = g // steps
 
         @pl.when(g % steps == 0)
         def _():
             pltpu.make_async_copy(held.at[h], held.at[h], in_recv.at[h]).wait()
-
-        @pl.when(g > 0)
-        def _():
-            give_block(g - 1)
 
         where = pl.ds(pl.multiple_of(far_first(g % steps) * pair, pair), pair)
         both = held[h, 0, where, :]
@@ -161,13 +158,19 @@
         moved = lax.dot_general(turned, values[:, :HEAD], NN, preferred_element_type=jnp.float32)
         result[h, where, :HEAD] = plain[:, :HEAD].astype(jnp.bfloat16)
         result[h, where, HEAD:] = (moved + plain[:, HEAD:]).astype(jnp.bfloat16)
+
+        @pl.when((g > 0) & (lax.rem(g + steps - 1, steps) < kept))
+        def _():
+            give_block(g - 1)
+
         return carry
 
-    last = per_group * steps - 1
-    lax.fori_loop(0, last + 1, block, 0)
+    lax.fori_loop(0, per_group * steps, block, 0)
     sent = held.at[:, :, pl.ds(0, (groups - 1) * rows), :]
     pltpu.make_async_copy(sent, sent, in_send).wait()
-    give_block(last)
+    for i in range(kept, steps):
+        for h in range(per_group):
+            give_block(h * steps + i)
     given = result.at[:, pl.ds(0, (groups - 1) * rows), :]
     pltpu.make_async_copy(given, given, out_send).wait()
     pltpu.make_async_copy(out_ref, out_ref, out_recv.at[0]).wait()

time: 190 us -> 190 us (level)
  no operation moved by 1% of the time
where the time goes in v4:
time: 190 us
  Pallas kernels  190 us (100%)
    pallas_call x1, Pallas kernels, on_device(): pl.pallas_call(functools.partial(kernel, groups), out_shape=(pltpu.VMEM(a...  188 us

profile of v4, /device:TPU:2, one launch (start us, length us, event | category | flops | bytes accessed | tf_op | source)
XLA Modules:
  0.0 190.3 jit_solution(17049021100749059827)
XLA Ops:
  0.6 188.3 %attention_tangent.1 = (bf16[128,4096]{1,0:T(8,128)(2,1)S(1)}, bf16[128,4096]{1,0:T(8,128)(2,1)S(1)}) custom-call(bf16[128,4096]{1,0:T(8,128)(2,1)} %q_ref.1, bf16[128,4096]{1,0:T(8,128)(2,1)} %k_ref.1, bf16[128,4096]{1,0:T(8,128)(2,1)} %v_ref.1, bf16[128,4096]{1,0:T(8,128)(2,1)} %dq_ref.1, bf16[128,4096]{1,0:T(8,128)(2,1)} %dk_ref.1, bf16[128,4096]{1,0:T(8,128)(2,1)} %dv_ref.1), custom_call_target="tpu_custom_call" | custom-call | tf_op jit(solution)/shard_map/attention_tangent/pallas_call | solution.py:196
  188.9 1.3 put_out.1

commit v5 on v4

--- a/solution.py
+++ b/solution.py
@@ -95,7 +95,7 @@
         for entry in plan:
 
             def send_rest(j, carry, h=h, entry=entry):
-                peer = far_first(j // 2) * 2 + lax.rem(my_y + j + 1, 2)
+                peer = far_first(lax.rem(j, steps)) * 2 + lax.rem(my_y + 1 + j // steps, 2)
                 send_to(h, peer, (entry,))
                 return carry
 

time: 190 us -> 190 us (level)
  no operation moved by 1% of the time
where the time goes in v5:
time: 190 us
  Pallas kernels  190 us (100%)
    pallas_call x1, Pallas kernels, on_device(): pl.pallas_call(functools.partial(kernel, groups), out_shape=(pltpu.VMEM(a...  188 us

profile of v5, /device:TPU:2, one launch (start us, length us, event | category | flops | bytes accessed | tf_op | source)
XLA Modules:
  0.0 190.3 jit_solution(11989775518323696303)
XLA Ops:
  0.6 188.3 %attention_tangent.1 = (bf16[128,4096]{1,0:T(8,128)(2,1)S(1)}, bf16[128,4096]{1,0:T(8,128)(2,1)S(1)}) custom-call(bf16[128,4096]{1,0:T(8,128)(2,1)} %q_ref.1, bf16[128,4096]{1,0:T(8,128)(2,1)} %k_ref.1, bf16[128,4096]{1,0:T(8,128)(2,1)} %v_ref.1, bf16[128,4096]{1,0:T(8,128)(2,1)} %dq_ref.1, bf16[128,4096]{1,0:T(8,128)(2,1)} %dk_ref.1, bf16[128,4096]{1,0:T(8,128)(2,1)} %dv_ref.1), custom_call_target="tpu_custom_call" | custom-call | tf_op jit(solution)/shard_map/attention_tangent/pallas_call | solution.py:196
  188.9 1.3 put_out.1
